TPU v7x, 512 devices: a whole 4x8x8 slice. The times are simulated.
512 devices in a mesh: seq: 256 (over x, y, z), head: 2 (over core).
Axes of the slice: x: 4, y: 8, z: 8, core: 2. Of those that a mesh axis runs over, the one named last changes fastest.
Arguments:
- queries: bfloat16 [49152, 2560], P('seq', 'head'), may hold values from -6 to 6
- keys: bfloat16 [49152, 2560], P('seq', 'head'), may hold values from -6 to 6
- values: bfloat16 [49152, 2560], P('seq', 'head'), may hold values from -6 to 6
- head_offsets: int32 [5, 20], P(None, 'head'), may hold values from 0 to 15, as said below
- norm_gain: float32 [2560], P('head'), may hold values from 0.1 to 1.9
Outputs:
- attended: bfloat16 [49152, 2560], P('seq', 'head')
- entropy: float32 [20, 49152], P('head', 'seq')
Inputs may be any that keep to these rules, and one draw needn't show every extreme that they name: head_offsets[k, h] lies in 0 to 2**k - 1; at each level some head has 2**k - 1.
All inputs are finite; a program needn't handle non-finite values.
Results may differ from a plain program's by a relative error of at most 0.004.
Values may be sent and summed in bfloat16 or wider, within the bound.
A program may use at most 64 MiB of HBM per device.

v0:
```python
import math

import jax
import jax.numpy as jnp
from jax import lax
from jax.sharding import PartitionSpec as P

DH = 128


def swapped(array, axis, apart):
    return lax.ppermute(array, axis, [(i, i ^ 1 << apart) for i in range(lax.axis_size(axis))])


def select_rows(heads_major, chosen, dilation):
    heads_here, tokens, width = heads_major.shape
    blocks = heads_major.reshape(heads_here, tokens // dilation, dilation, width)
    picked = jnp.einsum(
        "hnrd,hr->hnd", blocks, chosen.astype(jnp.bfloat16), preferred_element_type=jnp.float32
    )
    return picked.astype(jnp.bfloat16)


def attend(query_rows, key_rows, value_rows, logit_scale):
    scores = (
        jnp.einsum("hqd,hkd->hqk", query_rows, key_rows, preferred_element_type=jnp.float32)
        * logit_scale
    )
    row_peak = jnp.max(scores, axis=2)
    shifted = scores - row_peak[:, :, None]
    weights = jnp.exp(shifted)
    row_total = jnp.sum(weights, axis=2)
    spread = jnp.sum(weights * shifted, axis=2)
    weighted = jnp.einsum(
        "hqk,hkd->hqd", weights.astype(jnp.bfloat16), value_rows, preferred_element_type=jnp.float32
    )
    return (row_peak, row_total, spread, weighted)


def merge_level(running, parts, chosen):
    run_max, run_den, run_spread, run_out = running
    row_peak, row_total, spread, weighted = parts
    heads_here, tokens = run_max.shape
    count = row_peak.shape[1]
    dilation = chosen.shape[1]
    width = run_out.shape[2]
    run_max = run_max.reshape(heads_here, count, dilation)
    run_den = run_den.reshape(heads_here, count, dilation)
    run_spread = run_spread.reshape(heads_here, count, dilation)
    run_out = run_out.reshape(heads_here, count, dilation, width)
    present = chosen[:, None, :]
    level_peak = jnp.where(present, row_peak[:, :, None], run_max)
    new_max = jnp.maximum(run_max, level_peak)
    keep = jnp.exp(run_max - new_max)
    fresh = jnp.where(present, jnp.exp(level_peak - new_max), 0.0)
    denominator = run_den * keep + row_total[:, :, None] * fresh
    spread_sum = keep * (run_spread + (run_max - new_max) * run_den) + fresh * (
        spread[:, :, None] + (level_peak - new_max) * row_total[:, :, None]
    )
    output = run_out * keep[..., None] + weighted[:, :, None, :] * fresh[..., None]
    return (
        new_max.reshape(heads_here, tokens),
        denominator.reshape(heads_here, tokens),
        spread_sum.reshape(heads_here, tokens),
        output.reshape(heads_here, tokens, width),
    )


def near_first(paired, level_index):
    gathered = paired
    for bit_index in range(level_index):
        partner = swapped(gathered, "seq", bit_index)
        gathered = jnp.concatenate((gathered, partner), axis=2)
    return gathered


def shards(queries, keys, values, head_offsets, norm_gain):
    tokens = queries.shape[0]
    heads_here = head_offsets.shape[1]

    def heads_major(tensor):
        return tensor.reshape(tokens, heads_here, DH).transpose(1, 0, 2)

    query_major = heads_major(queries)
    key_major = heads_major(keys)
    value_major = heads_major(values)
    running = None
    for level_index in range(head_offsets.shape[0]):
        dilation = 2**level_index
        chosen = jnp.arange(dilation)[None, :] == head_offsets[level_index][:, None]
        logit_scale = math.log(tokens * dilation) / math.log(tokens) / math.sqrt(DH)
        if dilation == 1:
            query_sel, key_rows, value_rows = (query_major, key_major, value_major)
        else:
            query_sel = select_rows(query_major, chosen, dilation)
            key_sel = select_rows(key_major, chosen, dilation)
            value_sel = select_rows(value_major, chosen, dilation)
            paired = jnp.stack((key_sel, value_sel), axis=1)
            gathered = near_first(paired, level_index)
            key_rows = gathered[:, 0]
            value_rows = gathered[:, 1]
        parts = attend(query_sel, key_rows, value_rows, logit_scale)
        if running is None:
            running = parts
        else:
            running = merge_level(running, parts, chosen)
    run_max, run_den, run_spread, run_out = running
    output_major = run_out / run_den[:, :, None]
    entropy = jnp.log(run_den) - run_spread / run_den
    output = output_major.transpose(1, 0, 2).reshape(tokens, heads_here * DH)
    local_squares = jnp.sum(output * output, axis=1)
    total_squares = lax.psum(local_squares, "head")
    full_width = heads_here * DH * lax.axis_size("head")
    mean_square = (total_squares / full_width)[:, None]
    attended = (output * lax.rsqrt(mean_square + 1e-06) * norm_gain[None, :]).astype(jnp.bfloat16)
    return (attended, entropy)


def solution(mesh):
    in_specs = (P("seq", "head"), P("seq", "head"), P("seq", "head"), P(None, "head"), P("head"))
    out_specs = (P("seq", "head"), P("head", "seq"))
    return jax.shard_map(shards, mesh=mesh, in_specs=in_specs, out_specs=out_specs, check_vma=False)
```

profile of v0, /device:TPU:65, one launch (start us, length us, event | category | flops | bytes accessed | tf_op | source)
XLA Modules:
  0.0 160.0 jit_solution(4401003538188082768)
XLA Ops:
  0.6 0.8 slice_bitcast_fusion.19
  1.5 0.7 fusion.49
  2.1 1.3 copy.82
  5.4 1.9 %collective-permute-start.6 = (bf16[10,2,12,128]{3,2,0,1:T(8,128)(2,1)}, bf16[10,2,12,128]{3,2,0,1:T(8,128)(2,1)}, u32[]{:S(2)}, u32[]{:S(2)}) collective-permute-start(bf16[10,2,12,128]{3,2,0,1:T(8,128)(2,1)} %pad_maximum_fusion.12), channel_id=1, source_target_pairs={{0,2},{2,0},{4,6},{6,4},{8,10},{10,8},{12,14},{14,12},{16,18},{18,... | collective-permute-start | bytes 184328 | tf_op jit(solution)/shard_map/ppermute | solution.py:12
  7.3 0.7 iota_compare_fusion.1
  8.6 0.7 pad_maximum_fusion.10
  9.3 3.4 %collective-permute-start.3 = (bf16[10,2,24,128]{3,2,0,1:T(8,128)(2,1)}, bf16[10,2,24,128]{3,2,0,1:T(8,128)(2,1)}, u32[]{:S(2)}, u32[]{:S(2)}) collective-permute-start(bf16[10,2,24,128]{3,2,0,1:T(8,128)(2,1)} %pad_maximum_fusion.10), channel_id=1, source_target_pairs={{0,2},{2,0},{4,6},{6,4},{8,10},{10,8},{12,14},{14,12},{16,18},{18,... | collective-permute-start | bytes 368648 | tf_op jit(solution)/shard_map/ppermute | solution.py:12
  14.2 0.8 pad_maximum_fusion.7
  15.0 1.9 %collective-permute-start.1 = (bf16[10,2,48,128]{3,2,0,1:T(8,128)(2,1)}, bf16[10,2,48,128]{3,2,0,1:T(8,128)(2,1)}, u32[]{:S(2)}, u32[]{:S(2)}) collective-permute-start(bf16[10,2,48,128]{3,2,0,1:T(8,128)(2,1)} %pad_maximum_fusion.7), channel_id=1, source_target_pairs={{0,2},{2,0},{4,6},{6,4},{8,10},{10,8},{12,14},{14,12},{16,18},{18,... | collective-permute-start | bytes 737288 | tf_op jit(solution)/shard_map/ppermute | solution.py:12
  17.6 0.7 fusion.57
  19.0 0.9 pad_maximum_fusion.3
  19.9 3.3 %collective-permute-start = (bf16[10,2,96,128]{3,2,0,1:T(8,128)(2,1)}, bf16[10,2,96,128]{3,2,0,1:T(8,128)(2,1)}, u32[]{:S(2)}, u32[]{:S(2)}) collective-permute-start(bf16[10,2,96,128]{3,2,0,1:T(8,128)(2,1)} %pad_maximum_fusion.3), channel_id=1, source_target_pairs={{0,2},{2,0},{4,6},{6,4},{8,10},{10,8},{12,14},{14,12},{16,18},{18,... | collective-permute-start | bytes 1474568 | tf_op jit(solution)/shard_map/ppermute | solution.py:12
  23.5 1.0 copy.88
  25.6 0.9 fusion.24
  26.5 1.1 fusion.59
  27.6 1.4 fusion.56
  29.1 0.8 fusion.41
  29.9 1.0 pad_maximum_fusion.11
  30.9 5.8 %collective-permute-start.7 = (bf16[10,2,24,128]{3,2,0,1:T(8,128)(2,1)S(1)}, bf16[10,2,24,128]{3,2,0,1:T(8,128)(2,1)S(1)}, u32[]{:S(2)}, u32[]{:S(2)}) collective-permute-start(bf16[10,2,24,128]{3,2,0,1:T(8,128)(2,1)S(1)} %pad_maximum_fusion.11), channel_id=1, source_target_pairs={{0,4},{2,6},{4,0},{6,2},{8,12},{10,14},{12,8},{14,10},{16,20},{18,... | collective-permute-start | bytes 368648 | tf_op jit(solution)/shard_map/ppermute | solution.py:12
  36.7 1.6 %pad_maximum_fusion.8 = bf16[10,2,48,128]{3,2,0,1:T(8,128)(2,1)} fusion(bf16[10,2,24,128]{3,2,0,1:T(8,128)(2,1)} %collective-permute-done.3, bf16[10,1,24,128]{3,2,0,1:T(8,128)(2,1)S(1)} %copy-done.12, bf16[10,1,24,128]{3,2,0,1:T(8,128)(2,1)S(1)} %copy-done.15), kind=kLoop, calls=%fused_computation.67 | loop fusion | flops 737280 | bytes 491520 | tf_op jit(solution)/shard_map/concatenate | solution.py:73
  38.4 1.9 %collective-permute-start.4 = (bf16[10,2,48,128]{3,2,0,1:T(8,128)(2,1)}, bf16[10,2,48,128]{3,2,0,1:T(8,128)(2,1)S(1)}, u32[]{:S(2)}, u32[]{:S(2)}) collective-permute-start(bf16[10,2,48,128]{3,2,0,1:T(8,128)(2,1)} %pad_maximum_fusion.8), channel_id=1, source_target_pairs={{0,4},{2,6},{4,0},{6,2},{8,12},{10,14},{12,8},{14,10},{16,20},{18,... | collective-permute-start | bytes 737288 | tf_op jit(solution)/shard_map/ppermute | solution.py:12
  40.3 1.1 fusion
  41.4 0.7 broadcast_in_dim.171
  42.1 0.7 copy.99
  42.8 0.7 broadcast_in_dim.167
  43.7 0.7 copy.92
  44.3 1.0 pad_maximum_fusion.9
  45.3 8.2 %collective-permute-start.8 = (bf16[10,2,48,128]{3,2,0,1:T(8,128)(2,1)S(1)}, bf16[10,2,48,128]{3,2,0,1:T(8,128)(2,1)S(1)}, u32[]{:S(2)}, u32[]{:S(2)}) collective-permute-start(bf16[10,2,48,128]{3,2,0,1:T(8,128)(2,1)S(1)} %pad_maximum_fusion.9), channel_id=1, source_target_pairs={{0,8},{2,10},{4,12},{6,14},{8,0},{10,2},{12,4},{14,6},{16,24},{18,... | collective-permute-start | bytes 737288 | tf_op jit(solution)/shard_map/ppermute | solution.py:12
  53.6 1.8 %pad_maximum_fusion.4 = bf16[10,2,96,128]{3,2,0,1:T(8,128)(2,1)} fusion(bf16[10,2,48,128]{3,2,0,1:T(8,128)(2,1)} %collective-permute-done.1, bf16[10,1,48,128]{3,2,0,1:T(8,128)(2,1)S(1)} %copy-done.8, bf16[10,1,48,128]{3,2,0,1:T(8,128)(2,1)S(1)} %copy-done.10), kind=kLoop, calls=%fused_computation.52 | loop fusion | flops 1474560 | bytes 983040 | tf_op jit(solution)/shard_map/concatenate | solution.py:73
  55.3 7.3 %collective-permute-start.2 = (bf16[10,2,96,128]{3,2,0,1:T(8,128)(2,1)}, bf16[10,2,96,128]{3,2,0,1:T(8,128)(2,1)}, u32[]{:S(2)}, u32[]{:S(2)}) collective-permute-start(bf16[10,2,96,128]{3,2,0,1:T(8,128)(2,1)} %pad_maximum_fusion.4), channel_id=1, source_target_pairs={{0,4},{2,6},{4,0},{6,2},{8,12},{10,14},{12,8},{14,10},{16,20},{18,... | collective-permute-start | bytes 1474568 | tf_op jit(solution)/shard_map/ppermute | solution.py:12
  62.7 1.8 %pad_maximum_fusion.5 = bf16[10,2,96,128]{3,2,0,1:T(8,128)(2,1)} fusion(bf16[10,2,48,128]{3,2,0,1:T(8,128)(2,1)S(1)} %collective-permute-done.4, bf16[10,2,24,128]{3,2,0,1:T(8,128)(2,1)} %collective-permute-done.3, bf16[10,1,24,128]{3,2,0,1:T(8,128)(2,1)S(1)} %copy-done.12, bf16[10,1,24,128]{3,2,0,1:T(8,128)(2,1)S(1)} %copy-done.15), kind=kLoop, calls=%fused_computation.53 | loop fusion | flops 1966080 | bytes 983040 | tf_op jit(solution)/shard_map/concatenate | solution.py:73
  64.5 39.4 %collective-permute-start.5 = (bf16[10,2,96,128]{3,2,0,1:T(8,128)(2,1)}, bf16[10,2,96,128]{3,2,0,1:T(8,128)(2,1)}, u32[]{:S(2)}, u32[]{:S(2)}) collective-permute-start(bf16[10,2,96,128]{3,2,0,1:T(8,128)(2,1)} %pad_maximum_fusion.5), channel_id=1, source_target_pairs={{0,8},{2,10},{4,12},{6,14},{8,0},{10,2},{12,4},{14,6},{16,24},{18,... | collective-permute-start | bytes 1474568 | tf_op jit(solution)/shard_map/ppermute | solution.py:12
  103.9 1.8 %pad_maximum_fusion.6 = bf16[10,2,96,128]{3,2,0,1:T(8,128)(2,1)} fusion(bf16[10,2,48,128]{3,2,0,1:T(8,128)(2,1)S(1)} %collective-permute-done.8, bf16[10,2,24,128]{3,2,0,1:T(8,128)(2,1)S(1)} %collective-permute-done.7, bf16[10,2,12,128]{3,2,0,1:T(8,128)(2,1)} %collective-permute-done.6, bf16[10,1,12,128]{3,2,0,1:T(8,128)(2,1)S(1)} %copy-done.21, ...), kind=kLoop, calls=%fused_computation.54 | loop fusion | flops 2457600 | bytes 983040 | tf_op jit(solution)/shard_map/concatenate | solution.py:73
  105.8 3.5 %collective-permute-start.9 = (bf16[10,2,96,128]{3,2,0,1:T(8,128)(2,1)}, bf16[10,2,96,128]{3,2,0,1:T(8,128)(2,1)}, u32[]{:S(2)}, u32[]{:S(2)}) collective-permute-start(bf16[10,2,96,128]{3,2,0,1:T(8,128)(2,1)} %pad_maximum_fusion.6), channel_id=1, source_target_pairs={{0,16},{2,18},{4,20},{6,22},{8,24},{10,26},{12,28},{14,30},{16,0},... | collective-permute-start | bytes 1474568 | tf_op jit(solution)/shard_map/ppermute | solution.py:12
  109.3 1.1 pad_maximum_fusion
  110.5 1.0 copy-done.1
  112.8 0.7 copy.93
  113.6 0.7 copy.115
  114.4 0.7 copy.109
  115.1 2.2 %fusion.16 = f32[10,96,128]{2,1,0:T(8,128)} fusion(f32[10,96,192]{2,1,0:T(8,128)S(1)} %get-tuple-element.49, bf16[10,2,192,128]{3,2,0,1:T(8,128)(2,1)} %copy-done.1, f32[10,96]{1,0:T(8,128)S(1)} %get-tuple-element.48), kind=kOutput, calls=%fused_computation.39 | convolution fusion | flops 47554560 | bytes 1724160 | tf_op jit(solution)/shard_map/hqk,hkd->hqd/dot_general | solution.py:34
  117.3 1.2 pad_maximum_fusion.1
  119.0 0.7 copy.98
  119.7 0.9 fusion.15
  120.6 1.4 copy.116
  122.0 0.7 copy.110
  122.7 1.4 mul.440
  124.1 1.6 copy.111
  125.6 1.4 broadcast_in_dim.121
  127.0 1.6 copy.100
  128.6 1.4 add.189
  130.0 1.6 copy.118
  131.5 1.0 fusion.19
  132.6 1.3 pad_maximum_fusion.2
  134.7 0.7 add.195
  135.5 0.7 broadcast_in_dim.169
  136.3 0.7 mul.445
  137.1 1.0 fusion.18
  138.0 4.9 %concatenate.45 = bf16[10,2,192,128]{3,2,0,1:T(8,128)(2,1)S(1)} concatenate(bf16[10,2,12,128]{3,2,0,1:T(8,128)(2,1)} %pad_maximum_fusion.12, bf16[10,2,12,128]{3,2,0,1:T(8,128)(2,1)} %collective-permute-done.6, bf16[10,2,24,128]{3,2,0,1:T(8,128)(2,1)S(1)} %copy-done.17, bf16[10,2,48,128]{3,2,0,1:T(8,128)(2,1)} %copy-done.24, bf16[10,2,96,128]{3,2,0,1:T(8,128)(2,1)} %collective-permute-done.9), dimensions={2} | concatenate | bytes 1966080 | tf_op jit(solution)/shard_map/concatenate | solution.py:73
  144.2 0.8 broadcast_in_dim.172
  145.2 1.5 divide_subtract_fusion
  146.8 0.9 fusion.46
  148.8 4.6 %multiply_reduce_fusion.1 = (f32[192]{0:T(256)S(1)}, f32[192,10,128]{2,0,1:T(8,128)S(1)}) fusion(f32[10,192]{1,0:T(8,128)S(1)} %get-tuple-element.22, f32[10,192,128]{2,1,0:T(8,128)S(1)} %bitcast_multiply_fusion.1, f32[10,192]{1,0:T(8,128)S(1)} %get-tuple-element.21, f32[10,192]{1,0:T(8,128)S(1)} %get-tuple-element.27, f32[10,24,128]{2,1,0:T(8,128)S(1)} %copy-done.32, ...), kind=kOutput, calls=%fused_computation.32 | convolution fusion | flops 98918208 | bytes 6091008 | tf_op jit(solution)/shard_map/hqk,hkd->hqd/dot_general | solution.py:34
  153.4 5.0 %psum.7 = f32[192]{0:T(256)S(1)} all-reduce(f32[192]{0:T(256)S(1)} %get-tuple-element.52), channel_id=1, replica_groups=mesh['seq'=256,'head'=2] {'head'}, use_global_device_ids=true, to_apply=%region_11.12 | all-reduce | flops 192 | bytes 1536 | tf_op jit(solution)/shard_map/psum | solution.py:112
  159.0 1.0 copy.119
  (143 shorter events, 13.1 us)
Async XLA Ops:
  0.6 3.1 %copy-start.26 = (bf16[192,1280]{1,0:T(8,128)(2,1)S(1)}, bf16[192,1280]{1,0:T(8,128)(2,1)}, u32[]{:S(2)}) copy-start(bf16[192,1280]{1,0:T(8,128)(2,1)} %param.7) | copy-start | bytes 1474564
  4.0 4.6 %copy-start.2 = (bf16[192,1280]{0,1:T(8,128)(2,1)}, bf16[192,1280]{0,1:T(8,128)(2,1)S(1)}, u32[]{:S(2)}) copy-start(bf16[192,1280]{0,1:T(8,128)(2,1)S(1)} %copy.85) | copy-start | bytes 1474564
  4.7 3.8 %copy-start.18 = (bf16[10,1,12,128]{3,2,0,1:T(8,128)(2,1)}, bf16[10,1,12,128]{3,2,0,1:T(8,128)(2,1)S(1)}, u32[]{:S(2)}) copy-start(bf16[10,1,12,128]{3,2,0,1:T(8,128)(2,1)S(1)} %get-tuple-element.54) | copy-start | bytes 92164
  4.7 3.8 %copy-start.20 = (bf16[10,1,12,128]{3,2,0,1:T(8,128)(2,1)}, bf16[10,1,12,128]{3,2,0,1:T(8,128)(2,1)S(1)}, u32[]{:S(2)}) copy-start(bf16[10,1,12,128]{3,2,0,1:T(8,128)(2,1)S(1)} %get-tuple-element.55) | copy-start | bytes 92164
  5.4 24.5 %collective-permute-start.6 = (bf16[10,2,12,128]{3,2,0,1:T(8,128)(2,1)}, bf16[10,2,12,128]{3,2,0,1:T(8,128)(2,1)}, u32[]{:S(2)}, u32[]{:S(2)}) collective-permute-start(bf16[10,2,12,128]{3,2,0,1:T(8,128)(2,1)} %pad_maximum_fusion.12), channel_id=1, source_target_pairs={{0,2},{2,0},{4,6},{6,4},{8,10},{10,8},{12,14},{14,12},{16,18},{18,... | collective-permute-start | bytes 184328 | tf_op jit(solution)/shard_map/ppermute | solution.py:12
  8.6 9.6 %copy-start.11 = (bf16[10,1,24,128]{3,2,0,1:T(8,128)(2,1)}, bf16[10,1,24,128]{3,2,0,1:T(8,128)(2,1)S(1)}, u32[]{:S(2)}) copy-start(bf16[10,1,24,128]{3,2,0,1:T(8,128)(2,1)S(1)} %get-tuple-element.56) | copy-start | bytes 184324
  8.6 14.9 %copy-start.14 = (bf16[10,1,24,128]{3,2,0,1:T(8,128)(2,1)}, bf16[10,1,24,128]{3,2,0,1:T(8,128)(2,1)S(1)}, u32[]{:S(2)}) copy-start(bf16[10,1,24,128]{3,2,0,1:T(8,128)(2,1)S(1)} %get-tuple-element.57) | copy-start | bytes 184324
  9.3 27.4 %collective-permute-start.3 = (bf16[10,2,24,128]{3,2,0,1:T(8,128)(2,1)}, bf16[10,2,24,128]{3,2,0,1:T(8,128)(2,1)}, u32[]{:S(2)}, u32[]{:S(2)}) collective-permute-start(bf16[10,2,24,128]{3,2,0,1:T(8,128)(2,1)} %pad_maximum_fusion.10), channel_id=1, source_target_pairs={{0,2},{2,0},{4,6},{6,4},{8,10},{10,8},{12,14},{14,12},{16,18},{18,... | collective-permute-start | bytes 368648 | tf_op jit(solution)/shard_map/ppermute | solution.py:12
  14.2 4.8 %copy-start.7 = (bf16[10,1,48,128]{3,2,0,1:T(8,128)(2,1)}, bf16[10,1,48,128]{3,2,0,1:T(8,128)(2,1)S(1)}, u32[]{:S(2)}) copy-start(bf16[10,1,48,128]{3,2,0,1:T(8,128)(2,1)S(1)} %get-tuple-element.58) | copy-start | bytes 368644
  14.2 4.8 %copy-start.9 = (bf16[10,1,48,128]{3,2,0,1:T(8,128)(2,1)}, bf16[10,1,48,128]{3,2,0,1:T(8,128)(2,1)S(1)}, u32[]{:S(2)}) copy-start(bf16[10,1,48,128]{3,2,0,1:T(8,128)(2,1)S(1)} %get-tuple-element.59) | copy-start | bytes 368644
  15.0 38.6 %collective-permute-start.1 = (bf16[10,2,48,128]{3,2,0,1:T(8,128)(2,1)}, bf16[10,2,48,128]{3,2,0,1:T(8,128)(2,1)}, u32[]{:S(2)}, u32[]{:S(2)}) collective-permute-start(bf16[10,2,48,128]{3,2,0,1:T(8,128)(2,1)} %pad_maximum_fusion.7), channel_id=1, source_target_pairs={{0,2},{2,0},{4,6},{6,4},{8,10},{10,8},{12,14},{14,12},{16,18},{18,... | collective-permute-start | bytes 737288 | tf_op jit(solution)/shard_map/ppermute | solution.py:12
  17.6 1.4 copy-start.36
  18.3 5.0 %copy-start.27 = (bf16[192,1280]{1,0:T(8,128)(2,1)S(1)}, bf16[192,1280]{1,0:T(8,128)(2,1)}, u32[]{:S(2)}) copy-start(bf16[192,1280]{1,0:T(8,128)(2,1)} %param.5) | copy-start | bytes 1474564
  19.0 0.9 copy-start.4
  19.9 89.4 %collective-permute-start = (bf16[10,2,96,128]{3,2,0,1:T(8,128)(2,1)}, bf16[10,2,96,128]{3,2,0,1:T(8,128)(2,1)}, u32[]{:S(2)}, u32[]{:S(2)}) collective-permute-start(bf16[10,2,96,128]{3,2,0,1:T(8,128)(2,1)} %pad_maximum_fusion.3), channel_id=1, source_target_pairs={{0,2},{2,0},{4,6},{6,4},{8,10},{10,8},{12,14},{14,12},{16,18},{18,... | collective-permute-start | bytes 1474568 | tf_op jit(solution)/shard_map/ppermute | solution.py:12
  24.5 1.0 copy-start
  24.5 3.1 %copy-start.37 = (pred[10,2,1,1]{1,2,3,0:T(4,128)(4,1)S(1)}, pred[10,2,1,1]{1,2,3,0:T(4,128)(4,1)}, u32[]{:S(2)}) copy-start(pred[10,2,1,1]{1,2,3,0:T(4,128)(4,1)} %copy-done.36) | copy-start | bytes 64
  25.6 4.3 %copy-start.19 = (bf16[10,1,12,128]{3,2,0,1:T(8,128)(2,1)S(1)}, bf16[10,1,12,128]{3,2,0,1:T(8,128)(2,1)}, u32[]{:S(2)}) copy-start(bf16[10,1,12,128]{3,2,0,1:T(8,128)(2,1)} %copy-done.18) | copy-start | bytes 92164
  25.6 4.3 %copy-start.21 = (bf16[10,1,12,128]{3,2,0,1:T(8,128)(2,1)S(1)}, bf16[10,1,12,128]{3,2,0,1:T(8,128)(2,1)}, u32[]{:S(2)}) copy-start(bf16[10,1,12,128]{3,2,0,1:T(8,128)(2,1)} %copy-done.20) | copy-start | bytes 92164
  26.5 10.2 %copy-start.12 = (bf16[10,1,24,128]{3,2,0,1:T(8,128)(2,1)S(1)}, bf16[10,1,24,128]{3,2,0,1:T(8,128)(2,1)}, u32[]{:S(2)}) copy-start(bf16[10,1,24,128]{3,2,0,1:T(8,128)(2,1)} %copy-done.11) | copy-start | bytes 184324
  26.5 10.2 %copy-start.15 = (bf16[10,1,24,128]{3,2,0,1:T(8,128)(2,1)S(1)}, bf16[10,1,24,128]{3,2,0,1:T(8,128)(2,1)}, u32[]{:S(2)}) copy-start(bf16[10,1,24,128]{3,2,0,1:T(8,128)(2,1)} %copy-done.14) | copy-start | bytes 184324
  29.0 12.4 %copy-start.35 = (pred[10,16]{1,0:T(8,128)(4,1)S(1)}, pred[10,16]{1,0:T(8,128)(4,1)}, u32[]{:S(2)}) copy-start(pred[10,16]{1,0:T(8,128)(4,1)} %get-tuple-element.41) | copy-start | bytes 484
  29.0 13.1 %copy-start.39 = (pred[10,4]{0,1:T(4,128)(4,1)S(1)}, pred[10,4]{0,1:T(4,128)(4,1)}, u32[]{:S(2)}) copy-start(pred[10,4]{0,1:T(4,128)(4,1)} %get-tuple-element.34) | copy-start | bytes 124
  29.0 13.8 %copy-start.34 = (pred[10,8]{1,0:T(8,128)(4,1)S(1)}, pred[10,8]{1,0:T(8,128)(4,1)}, u32[]{:S(2)}) copy-start(pred[10,8]{1,0:T(8,128)(4,1)} %get-tuple-element.38) | copy-start | bytes 244
  29.1 14.5 %copy-start.38 = (pred[10,2]{0,1:T(4,128)(4,1)S(1)}, pred[10,2]{0,1:T(4,128)(4,1)}, u32[]{:S(2)}) copy-start(pred[10,2]{0,1:T(4,128)(4,1)} %get-tuple-element.36) | copy-start | bytes 64
  29.9 23.7 %copy-start.8 = (bf16[10,1,48,128]{3,2,0,1:T(8,128)(2,1)S(1)}, bf16[10,1,48,128]{3,2,0,1:T(8,128)(2,1)}, u32[]{:S(2)}) copy-start(bf16[10,1,48,128]{3,2,0,1:T(8,128)(2,1)} %copy-done.7) | copy-start | bytes 368644
  29.9 23.7 %copy-start.10 = (bf16[10,1,48,128]{3,2,0,1:T(8,128)(2,1)S(1)}, bf16[10,1,48,128]{3,2,0,1:T(8,128)(2,1)}, u32[]{:S(2)}) copy-start(bf16[10,1,48,128]{3,2,0,1:T(8,128)(2,1)} %copy-done.9) | copy-start | bytes 368644
  30.9 13.5 %collective-permute-start.7 = (bf16[10,2,24,128]{3,2,0,1:T(8,128)(2,1)S(1)}, bf16[10,2,24,128]{3,2,0,1:T(8,128)(2,1)S(1)}, u32[]{:S(2)}, u32[]{:S(2)}) collective-permute-start(bf16[10,2,24,128]{3,2,0,1:T(8,128)(2,1)S(1)} %pad_maximum_fusion.11), channel_id=1, source_target_pairs={{0,4},{2,6},{4,0},{6,2},{8,12},{10,14},{12,8},{14,10},{16,20},{18,... | collective-permute-start | bytes 368648 | tf_op jit(solution)/shard_map/ppermute | solution.py:12
  38.4 24.3 %collective-permute-start.4 = (bf16[10,2,48,128]{3,2,0,1:T(8,128)(2,1)}, bf16[10,2,48,128]{3,2,0,1:T(8,128)(2,1)S(1)}, u32[]{:S(2)}, u32[]{:S(2)}) collective-permute-start(bf16[10,2,48,128]{3,2,0,1:T(8,128)(2,1)} %pad_maximum_fusion.8), channel_id=1, source_target_pairs={{0,4},{2,6},{4,0},{6,2},{8,12},{10,14},{12,8},{14,10},{16,20},{18,... | collective-permute-start | bytes 737288 | tf_op jit(solution)/shard_map/ppermute | solution.py:12
  41.4 67.9 %copy-start.5 = (bf16[10,1,96,128]{3,2,0,1:T(8,128)(2,1)S(1)}, bf16[10,1,96,128]{3,2,0,1:T(8,128)(2,1)}, u32[]{:S(2)}) copy-start(bf16[10,1,96,128]{3,2,0,1:T(8,128)(2,1)} %copy-done.4) | copy-start | bytes 737284
  44.3 66.1 %copy-start.16 = (bf16[10,2,24,128]{3,2,0,1:T(8,128)(2,1)}, bf16[10,2,24,128]{3,2,0,1:T(8,128)(2,1)S(1)}, u32[]{:S(2)}) copy-start(bf16[10,2,24,128]{3,2,0,1:T(8,128)(2,1)S(1)} %collective-permute-done.7) | copy-start | bytes 368644
  45.3 58.6 %collective-permute-start.8 = (bf16[10,2,48,128]{3,2,0,1:T(8,128)(2,1)S(1)}, bf16[10,2,48,128]{3,2,0,1:T(8,128)(2,1)S(1)}, u32[]{:S(2)}, u32[]{:S(2)}) collective-permute-start(bf16[10,2,48,128]{3,2,0,1:T(8,128)(2,1)S(1)} %pad_maximum_fusion.9), channel_id=1, source_target_pairs={{0,8},{2,10},{4,12},{6,14},{8,0},{10,2},{12,4},{14,6},{16,24},{18,... | collective-permute-start | bytes 737288 | tf_op jit(solution)/shard_map/ppermute | solution.py:12
  55.3 56.1 %copy-start.28 = (f32[10,1,96,128]{3,1,2,0:T(1,128)S(1)}, f32[10,1,96,128]{3,1,2,0:T(1,128)}, u32[]{:S(2)}) copy-start(f32[10,1,96,128]{3,1,2,0:T(1,128)} %fusion.56) | copy-start | bytes 1474564
  55.3 62.0 %collective-permute-start.2 = (bf16[10,2,96,128]{3,2,0,1:T(8,128)(2,1)}, bf16[10,2,96,128]{3,2,0,1:T(8,128)(2,1)}, u32[]{:S(2)}, u32[]{:S(2)}) collective-permute-start(bf16[10,2,96,128]{3,2,0,1:T(8,128)(2,1)} %pad_maximum_fusion.4), channel_id=1, source_target_pairs={{0,4},{2,6},{4,0},{6,2},{8,12},{10,14},{12,8},{14,10},{16,20},{18,... | collective-permute-start | bytes 1474568 | tf_op jit(solution)/shard_map/ppermute | solution.py:12
  62.7 47.8 %copy-start.23 = (bf16[10,2,48,128]{3,2,0,1:T(8,128)(2,1)}, bf16[10,2,48,128]{3,2,0,1:T(8,128)(2,1)S(1)}, u32[]{:S(2)}) copy-start(bf16[10,2,48,128]{3,2,0,1:T(8,128)(2,1)S(1)} %collective-permute-done.4) | copy-start | bytes 737284
  64.5 68.1 %collective-permute-start.5 = (bf16[10,2,96,128]{3,2,0,1:T(8,128)(2,1)}, bf16[10,2,96,128]{3,2,0,1:T(8,128)(2,1)}, u32[]{:S(2)}, u32[]{:S(2)}) collective-permute-start(bf16[10,2,96,128]{3,2,0,1:T(8,128)(2,1)} %pad_maximum_fusion.5), channel_id=1, source_target_pairs={{0,8},{2,10},{4,12},{6,14},{8,0},{10,2},{12,4},{14,6},{16,24},{18,... | collective-permute-start | bytes 1474568 | tf_op jit(solution)/shard_map/ppermute | solution.py:12
  103.9 5.4 %copy-start.24 = (bf16[10,2,48,128]{3,2,0,1:T(8,128)(2,1)}, bf16[10,2,48,128]{3,2,0,1:T(8,128)(2,1)S(1)}, u32[]{:S(2)}) copy-start(bf16[10,2,48,128]{3,2,0,1:T(8,128)(2,1)S(1)} %collective-permute-done.8) | copy-start | bytes 737284
  105.8 32.2 %collective-permute-start.9 = (bf16[10,2,96,128]{3,2,0,1:T(8,128)(2,1)}, bf16[10,2,96,128]{3,2,0,1:T(8,128)(2,1)}, u32[]{:S(2)}, u32[]{:S(2)}) collective-permute-start(bf16[10,2,96,128]{3,2,0,1:T(8,128)(2,1)} %pad_maximum_fusion.6), channel_id=1, source_target_pairs={{0,16},{2,18},{4,20},{6,22},{8,24},{10,26},{12,28},{14,30},{16,0},... | collective-permute-start | bytes 1474568 | tf_op jit(solution)/shard_map/ppermute | solution.py:12
  110.5 1.0 copy-start.1
  115.1 3.4 %copy-start.29 = (f32[10,1,48,128]{3,1,2,0:T(1,128)S(1)}, f32[10,1,48,128]{3,1,2,0:T(1,128)}, u32[]{:S(2)}) copy-start(f32[10,1,48,128]{3,1,2,0:T(1,128)} %fusion.59) | copy-start | bytes 737284
  118.5 14.1 %copy-start.13 = (bf16[10,1,24,128]{3,2,0,1:T(8,128)(2,1)S(1)}, bf16[10,1,24,128]{3,2,0,1:T(8,128)(2,1)}, u32[]{:S(2)}) copy-start(bf16[10,1,24,128]{3,2,0,1:T(8,128)(2,1)} %copy-done.11) | copy-start | bytes 184324
  131.5 2.4 %copy-start.25 = (f32[10,1,24,128]{3,1,2,0:T(1,128)S(1)}, f32[10,1,24,128]{3,1,2,0:T(1,128)}, u32[]{:S(2)}) copy-start(f32[10,1,24,128]{3,1,2,0:T(1,128)} %fusion.24) | copy-start | bytes 368644
  132.6 5.4 %copy-start.17 = (bf16[10,2,24,128]{3,2,0,1:T(8,128)(2,1)S(1)}, bf16[10,2,24,128]{3,2,0,1:T(8,128)(2,1)}, u32[]{:S(2)}) copy-start(bf16[10,2,24,128]{3,2,0,1:T(8,128)(2,1)} %copy-done.16) | copy-start | bytes 368644
  134.4 8.6 %copy-start.30 = (bf16[10,1,12,128]{3,1,2,0:T(2,128)(2,1)S(1)}, bf16[10,1,12,128]{3,1,2,0:T(2,128)(2,1)}, u32[]{:S(2)}) copy-start(bf16[10,1,12,128]{3,1,2,0:T(2,128)(2,1)} %fusion.41) | copy-start | bytes 92164
  143.0 5.0 %copy-start.6 = (f32[10,96,128]{2,1,0:T(8,128)S(1)}, f32[10,96,128]{2,1,0:T(8,128)}, u32[]{:S(2)}) copy-start(f32[10,96,128]{2,1,0:T(8,128)} %fusion.16) | copy-start | bytes 1474564
  143.4 0.6 copy-start.31
  143.7 4.6 %copy-start.22 = (f32[10,48,128]{2,1,0:T(8,128)S(1)}, f32[10,48,128]{2,1,0:T(8,128)}, u32[]{:S(2)}) copy-start(f32[10,48,128]{2,1,0:T(8,128)} %fusion.19) | copy-start | bytes 737284
  147.7 1.1 copy-start.3
  147.7 1.1 copy-start.32
  153.4 5.4 %copy-start.33 = (f32[1280]{0:T(1024)S(1)}, f32[1280]{0:T(1024)}, u32[]{:S(2)}) copy-start(f32[1280]{0:T(1024)} %param.9) | copy-start | bytes 15364
where the time goes:
time: 162 us; the launch traced here: 160 us
  starting transfers between devices  76.7 us (47%)
  local copies, waits for them, and re-layouts  33.9 us (21%)
  other arithmetic  24.1 us (15%)
  matrix products  18.9 us (12%)
  blocking collectives  4.96 us (3%)
    ppermute x10, starting transfers between devices, swapped(): lax.ppermute(array, axis, [(i, i ^ 1 << apart) for i in range(lax.axis_si...  76.7 us
    concatenate x9, other arithmetic, near_first(): gathered = jnp.concatenate((gathered, partner), axis=2)  12.6 us
    dot_general x5, matrix products, attend(): jnp.einsum('hqk,hkd->hqd', weights.astype(jnp.bfloat16), value_rows, pref...  9.15 us
    broadcast_in_dim x17, local copies, waits for them, and re-layouts, merge_level(): level_peak = jnp.where(present, row_peak[:, :, None], run_max)  8.24 us
    dot_general x12, matrix products, select_rows(): jnp.einsum('hnrd,hr->hnd', blocks, chosen.astype(jnp.bfloat16), preferred...  7.38 us
    psum x1, blocking collectives, shards(): total_squares = lax.psum(local_squares, 'head')  4.96 us
    concatenate x1, local copies, waits for them, and re-layouts, near_first(): gathered = jnp.concatenate((gathered, partner), axis=2)  4.92 us
    unnamed x84, local copies, waits for them, and re-layouts  4.65 us
  transfers between devices with their start and end apart: 10, of which 0 were waited for; matrix products, arithmetic and copies ran while one was open for 34% of the time, Pallas kernels for 0%

commit v1 on v0

v1 whole, which is shorter than its diff:
```python
import math

import jax
import jax.numpy as jnp
from jax import lax
from jax.experimental import pallas as pl
from jax.experimental.pallas import tpu as pltpu
from jax.sharding import PartitionSpec as P

DH = 128
TOK = 192
HEADS = 10
LEVELS = 5
MESH = pl.DeviceIdType.MESH
F32 = jnp.float32
BF16 = jnp.bfloat16
SLOTS = {2: 3, 3: 2, 4: 1}
PACK = {2: 144, 3: 80, 4: 48}
BACK = {2: 64, 3: 48, 4: 32}
OUT_ROWS = {2: 48, 3: 32, 4: 16}


def scale_of(level):
    return math.log(TOK * 2**level) / math.log(TOK) / math.sqrt(DH)


def dot(a, b, dims):
    return lax.dot_general(a, b, (dims, ((), ())), preferred_element_type=F32)


def pick(level, offset, rows):
    row = lax.broadcasted_iota(jnp.int32, (rows, TOK), 0)
    token = lax.broadcasted_iota(jnp.int32, (rows, TOK), 1)
    return jnp.where(token == row * 2**level + offset, 1.0, 0.0).astype(F32)


def soft(keys, queries, level):
    scores = dot(keys, queries, ((1,), (1,))) * scale_of(level)
    peak = jnp.max(scores, axis=0, keepdims=True)
    shifted = scores - peak
    weights = jnp.exp(shifted)
    total = jnp.sum(weights, axis=0, keepdims=True)
    spread = jnp.sum(weights * shifted, axis=0, keepdims=True)
    return peak, total, spread, weights.astype(BF16)


def thirds(value):
    high = value.astype(BF16).astype(F32)
    rest = value - high
    middle = rest.astype(BF16).astype(F32)
    return high, middle, rest - middle


def stat_rows(stats):
    width = stats[0].shape[1]
    row = lax.broadcasted_iota(jnp.int32, (16, width), 0)
    result = jnp.zeros((16, width), F32)
    for place, stat in enumerate(stats):
        for part, piece in enumerate(thirds(stat)):
            result = jnp.where(row == 3 * part + place, piece, result)
    return result


def stat_values(rows):
    return tuple(
        rows[6 + i : 7 + i] + rows[3 + i : 4 + i] + rows[i : i + 1] for i in range(3)
    )


def kernel(
    offs, q_ref, k_ref, v_ref, gain_ref, out_ref, ent_ref,
    send1, send2, send3, send4, recv1, recv2, recv3, recv4, query1,
    back2, back3, back4, ret2, ret3, ret4, stats, merged, plain, squares, others,
    s1, s2, s3, s4, r1, r2, r3, r4, t2, t3, t4, u2, u3, u4, sq_sem,
):
    send, recv, back, ret = (
        {2: send2, 3: send3, 4: send4},
        {2: recv2, 3: recv3, 4: recv4},
        {2: back2, 3: back3, 4: back4},
        {2: ret2, 3: ret3, 4: ret4},
    )
    send_sem, recv_sem, back_sem, ret_sem = (
        {2: s2, 3: s3, 4: s4},
        {2: r2, 3: r3, 4: r4},
        {2: t2, 3: t3, 4: t4},
        {2: u2, 3: u3, 4: u4},
    )
    seq = lax.axis_index("seq")
    core = lax.axis_index("head")

    barrier = pltpu.get_barrier_semaphore()
    mine16 = lax.rem(seq, 16)
    for step in range(1, 16):
        peer = seq - mine16 + lax.rem(mine16 + step, 16)
        pl.semaphore_signal(barrier, inc=1, device_id={"seq": peer, "head": core}, device_id_type=MESH)
    pl.semaphore_signal(barrier, inc=1, device_id={"seq": seq, "head": 1 - core}, device_id_type=MESH)

    def columns(h):
        return pl.ds(pl.multiple_of(h * DH, DH), DH)

    @pl.loop(0, HEADS)
    def _(h):
        chosen = jnp.concatenate(
            [pick(1, offs[1, h], 96), pick(2, offs[2, h], 48), pick(3, offs[3, h], 24), pick(4, offs[4, h], 24)],
            axis=0,
        ).astype(BF16)
        keys = dot(chosen, k_ref[:, columns(h)], ((1,), (0,)))
        vals = dot(chosen, v_ref[:, columns(h)], ((1,), (0,)))
        ques = dot(chosen, q_ref[:, columns(h)], ((1,), (0,)))
        send1[h, 0:96] = keys[0:96].astype(BF16)
        send1[h, 96:192] = vals[0:96].astype(BF16)
        query1[h] = ques[0:96].astype(BF16)
        send2[h] = jnp.concatenate([a[96:144] for a in (keys, vals, ques)], axis=0).astype(BF16)
        send3[h] = jnp.concatenate(
            [a[144:168] for a in (keys, vals, ques)] + [jnp.zeros((8, DH), F32)], axis=0
        ).astype(BF16)
        send4[h] = jnp.concatenate([a[168:184] for a in (keys, vals, ques)], axis=0).astype(BF16)

    pl.semaphore_wait(barrier, 16)

    def member(level):
        return lax.rem(seq, 2**level)

    def flip(level, order):
        return order + core * (2**level - 1 - 2 * order)

    def owner(level, h):
        return flip(level, lax.rem(h, 2**level))

    def pack_copy(level, h):
        return pltpu.make_async_remote_copy(
            src_ref=send[level].at[h],
            dst_ref=recv[level].at[h // 2**level, member(level)],
            send_sem=send_sem[level].at[h],
            recv_sem=recv_sem[level].at[h // 2**level, member(level)],
            device_id={"seq": seq - member(level) + owner(level, h), "head": core},
            device_id_type=MESH,
        )

    def near_copy(h):
        return pltpu.make_async_remote_copy(
            src_ref=send1.at[h],
            dst_ref=recv1.at[h],
            send_sem=s1.at[h],
            recv_sem=r1.at[h],
            device_id={"seq": seq + 1 - 2 * lax.rem(seq, 2), "head": core},
            device_id_type=MESH,
        )

    def back_copy(level, slot, m):
        return pltpu.make_async_remote_copy(
            src_ref=back[level].at[slot, m],
            dst_ref=ret[level].at[flip(level, member(level)) + slot * 2**level],
            send_sem=back_sem[level].at[slot, m],
            recv_sem=ret_sem[level].at[flip(level, member(level)) + slot * 2**level],
            device_id={"seq": seq - member(level) + m, "head": core},
            device_id_type=MESH,
        )

    for level in (2, 3, 4):

        @pl.loop(0, HEADS)
        def _(h):
            @pl.when(owner(level, h) != member(level))
            def _():
                pack_copy(level, h).start()

            @pl.when(owner(level, h) == member(level))
            def _():
                recv[level][h // 2**level, member(level)] = send[level][h]

    @pl.loop(0, HEADS)
    def _(h):
        near_copy(h).start()

    @pl.loop(0, HEADS)
    def _(h):
        peak, total, spread, weights = soft(k_ref[:, columns(h)], q_ref[:, columns(h)], 0)
        stats[h, 0:1] = peak
        stats[h, 1:2] = total
        stats[h, 2:3] = spread
        merged[h] = dot(v_ref[:, columns(h)], weights, ((0,), (0,)))

    for level in (2, 3, 4):
        group = 2**level
        rows = TOK // group
        for slot in range(SLOTS[level]):
            held = flip(level, member(level)) + slot * group

            @pl.when(held < HEADS)
            def _():
                for m in range(group):

                    @pl.when(m != member(level))
                    def _():
                        pltpu.make_async_copy(
                            send[level].at[0], recv[level].at[slot, m], recv_sem[level].at[slot, m]
                        ).wait()

                if level == 4:
                    line = lax.broadcasted_iota(jnp.int32, (TOK, 256), 0)
                    place = lax.broadcasted_iota(jnp.int32, (TOK, 256), 1)
                    within = place & 15
                    dense = jnp.where(
                        ((place >> 4) * 12 + within == line) & (within < 12), 1.0, 0.0
                    ).astype(BF16)
                    tall = [
                        jnp.concatenate([recv4[slot, m, 16 * i : 16 * i + 16] for m in range(group)], axis=0)
                        for i in range(3)
                    ]
                    keys = dot(dense, tall[0], ((1,), (0,))).astype(BF16)
                    vals = dot(dense, tall[1], ((1,), (0,))).astype(BF16)
                    ques = tall[2]
                    per = 16
                elif level == 3:
                    wide = [recv3[slot, m].astype(F32) for m in range(group)]
                    keys, vals, ques = (
                        jnp.concatenate([w[rows * i : rows * i + rows] for w in wide], axis=0).astype(BF16)
                        for i in range(3)
                    )
                    per = rows
                else:
                    keys, vals, ques = (
                        jnp.concatenate([recv2[slot, m, rows * i : rows * i + rows] for m in range(group)], axis=0)
                        for i in range(3)
                    )
                    per = rows
                peak, total, spread, weights = soft(keys, ques, level)
                partial = dot(weights, vals, ((0,), (0,)))
                lines = stat_rows((peak, total, spread))
                if lines.shape[1] < 256:
                    lines = jnp.concatenate([lines, jnp.zeros((16, 256 - lines.shape[1]), F32)], axis=1)
                for m in range(group):
                    turned = lines if m == 0 else pltpu.roll(lines, 256 - m * per, 1)
                    pieces = [partial[m * per : m * per + per]]
                    if level == 3:
                        pieces.append(jnp.zeros((8, DH), F32))
                    pieces.append(turned[:, 0:DH])
                    back[level][slot, m] = jnp.concatenate(pieces, axis=0).astype(BF16)
                for m in range(group):

                    @pl.when(m != member(level))
                    def _():
                        back_copy(level, slot, m).start()

                    @pl.when(m == member(level))
                    def _():
                        ret[level][held] = back[level][slot, m]

    def state(h):
        return stats[h, 0:1], stats[h, 1:2], stats[h, 2:3]

    token = lax.broadcasted_iota(jnp.int32, (1, TOK), 1)

    def present(level, h):
        return (token & (2**level - 1)) == offs[level, h]

    @pl.loop(0, HEADS)
    def _(h):
        near_copy(h).wait_recv()
        keys = jnp.concatenate([send1[h, 0:96], recv1[h, 0:96]], axis=0)
        vals = jnp.concatenate([send1[h, 96:192], recv1[h, 96:192]], axis=0)
        peak, total, spread, weights = soft(keys, query1[h], 1)
        partial = dot(vals, weights, ((0,), (0,)))
        high = partial.astype(BF16)
        low = (partial - high.astype(F32)).astype(BF16)
        lines = stat_rows((peak, total, spread)).astype(BF16)
        spots = pick(1, offs[1, h], 96).astype(BF16)
        wide = dot(jnp.concatenate([high, low, lines], axis=0), spots, ((1,), (0,)))
        peak, total, spread = stat_values(wide[2 * DH : 2 * DH + 16])
        there = present(1, h)
        top, mass, moment = state(h)
        peak = jnp.where(there, peak, top)
        new = jnp.maximum(top, peak)
        keep = jnp.exp(top - new)
        fresh = jnp.where(there, jnp.exp(peak - new), 0.0)
        stats[h, 0:1] = new
        stats[h, 1:2] = mass * keep + total * fresh
        stats[h, 2:3] = keep * (moment + (top - new) * mass) + fresh * (spread + (peak - new) * total)
        merged[h] = merged[h] * keep + (wide[0:DH] + wide[DH : 2 * DH]) * fresh

    squares[...] = jnp.zeros_like(squares)

    @pl.loop(0, HEADS)
    def _(h):
        for level in (2, 3, 4):

            @pl.when(owner(level, h) != member(level))
            def _():
                pltpu.make_async_copy(back[level].at[0, 0], ret[level].at[h], ret_sem[level].at[h]).wait()

        top, mass, moment = state(h)
        new = top
        found = []
        for level in (2, 3, 4):
            count = OUT_ROWS[level]
            spots = pick(level, offs[level, h], DH).astype(BF16)
            lines = dot(ret[level][h, count : count + 16], spots, ((1,), (0,)))
            peak, total, spread = stat_values(lines)
            there = present(level, h)
            peak = jnp.where(there, peak, top)
            new = jnp.maximum(new, peak)
            part = dot(ret[level][h, 0:count], spots[0:count], ((0,), (0,)))
            found.append((there, peak, total, spread, part))
        keep = jnp.exp(top - new)
        weight = mass * keep
        sway = keep * (moment + (top - new) * mass)
        factors = []
        for there, peak, total, spread, part in found:
            fresh = jnp.where(there, jnp.exp(peak - new), 0.0)
            weight = weight + total * fresh
            sway = sway + fresh * (spread + (peak - new) * total)
            factors.append(fresh)
        ent_ref[pl.ds(h, 1), :] = jnp.log(weight) - sway / weight
        output = merged[h] * keep
        for (there, peak, total, spread, part), fresh in zip(found, factors):
            output = output + part * fresh
        output = output * (1.0 / weight)
        squares[0:1] += jnp.sum(output * output, axis=0, keepdims=True)
        plain[:, columns(h)] = jnp.transpose(output)

    swap = pltpu.make_async_remote_copy(
        src_ref=squares,
        dst_ref=others,
        send_sem=sq_sem.at[0],
        recv_sem=sq_sem.at[1],
        device_id={"seq": seq, "head": 1 - core},
        device_id_type=MESH,
    )
    swap.start()

    @pl.loop(0, HEADS)
    def _(h):
        near_copy(h).wait_send()
        for level in (2, 3, 4):

            @pl.when(owner(level, h) != member(level))
            def _():
                pack_copy(level, h).wait_send()

    for level in (2, 3, 4):
        for slot in range(SLOTS[level]):

            @pl.when(flip(level, member(level)) + slot * 2**level < HEADS)
            def _():
                for m in range(2**level):

                    @pl.when(m != member(level))
                    def _():
                        back_copy(level, slot, m).wait_send()

    swap.wait()
    square = (squares[0:1] + others[0:1]) / (2 * HEADS * DH)
    factor = lax.rsqrt(square + 1e-06)
    factor = jnp.transpose(jnp.broadcast_to(factor, (DH, TOK)))

    @pl.loop(0, HEADS)
    def _(h):
        out_ref[:, columns(h)] = (plain[:, columns(h)] * factor * gain_ref[:, columns(h)]).astype(BF16)


def shards(queries, keys, values, head_offsets, norm_gain):
    vmem = pl.BlockSpec(memory_space=pltpu.VMEM)
    smem = pl.BlockSpec(memory_space=pltpu.SMEM)
    dma = pltpu.SemaphoreType.DMA

    def buffers(shape_of):
        return [pltpu.VMEM(shape_of(level), BF16) for level in (2, 3, 4)]

    scratch = [pltpu.VMEM((HEADS, TOK, DH), BF16)]
    scratch += buffers(lambda k: (HEADS, PACK[k], DH))
    scratch += [pltpu.VMEM((HEADS, TOK, DH), BF16)]
    scratch += buffers(lambda k: (SLOTS[k], 2**k, PACK[k], DH))
    scratch += [pltpu.VMEM((HEADS, TOK // 2, DH), BF16)]
    scratch += buffers(lambda k: (SLOTS[k], 2**k, BACK[k], DH))
    scratch += buffers(lambda k: (HEADS, BACK[k], DH))
    scratch += [
        pltpu.VMEM((HEADS, 8, TOK), F32),
        pltpu.VMEM((HEADS, DH, TOK), F32),
        pltpu.VMEM((TOK, HEADS * DH), F32),
        pltpu.VMEM((8, TOK), F32),
        pltpu.VMEM((8, TOK), F32),
    ]
    scratch += [dma((HEADS,)) for _ in range(5)]
    scratch += [dma((SLOTS[k], 2**k)) for k in (2, 3, 4)]
    scratch += [dma((SLOTS[k], 2**k)) for k in (2, 3, 4)]
    scratch += [dma((HEADS,)) for _ in range(3)]
    scratch += [dma((2,))]
    return pl.pallas_call(
        kernel,
        out_shape=(
            jax.ShapeDtypeStruct((TOK, HEADS * DH), BF16),
            jax.ShapeDtypeStruct((HEADS, TOK), F32),
        ),
        in_specs=[smem, vmem, vmem, vmem, vmem],
        out_specs=(vmem, vmem),
        scratch_shapes=scratch,
        compiler_params=pltpu.CompilerParams(collective_id=0, has_side_effects=True),
        name="dilated",
    )(head_offsets, queries, keys, values, norm_gain.reshape(1, HEADS * DH))


def solution(mesh):
    in_specs = (P("seq", "head"), P("seq", "head"), P("seq", "head"), P(None, "head"), P("head"))
    out_specs = (P("seq", "head"), P("head", "seq"))
    return jax.shard_map(shards, mesh=mesh, in_specs=in_specs, out_specs=out_specs, check_vma=False)
```

time: 162 us -> 58.1 us (0.36)
  the two profiles are of different devices: /device:TPU:65 before, /device:TPU:1 now
where the time goes in v1:
time: 58.1 us; the launch traced here: 57.9 us
  Pallas kernels  53.5 us (92%)
  local copies, waits for them, and re-layouts  3.75 us (6%)
  between operations  0.65 us (1%)
    pallas_call x1, Pallas kernels, shards(): pl.pallas_call(kernel, out_shape=(jax.ShapeDtypeStruct((TOK, HEADS * DH),...  53.5 us
    unnamed x4, local copies, waits for them, and re-layouts  2.45 us
    reshape x1, local copies, waits for them, and re-layouts, shards(): norm_gain.reshape(1, HEADS * DH)  1.29 us

profile of v1, /device:TPU:1, one launch (start us, length us, event | category | flops | bytes accessed | tf_op | source)
XLA Modules:
  0.0 57.9 jit_solution(18110443534604272341)
XLA Ops:
  0.6 1.3 %reshape.7.gain_ref = f32[1,1280]{1,0:T(1,128)} reshape(f32[1280]{0:T(1024)} %param.9) | data formatting | bytes 10240 | tf_op jit(solution)/shard_map/reshape | solution.py:400
  1.9 53.5 %dilated.1 = (bf16[192,1280]{1,0:T(8,128)(2,1)}, f32[10,192]{1,0:T(8,128)}) custom-call(s32[5,10]{1,0:T(8,128)} %offs.1, bf16[192,1280]{1,0:T(8,128)(2,1)} %q_ref.1, bf16[192,1280]{1,0:T(8,128)(2,1)} %k_ref.1, bf16[192,1280]{1,0:T(8,128)(2,1)} %v_ref.1, f32[1,1280]{1,0:T(1,128)} %reshape.7.gain_ref), custom_call_target="tpu_custom_call" | custom-call | tf_op jit(solution)/shard_map/dilated/pallas_call | solution.py:389
  55.4 0.0 copy-start
  55.4 1.8 %copy.9 = bf16[192,1280]{1,0:T(8,128)(2,1)} copy(bf16[192,1280]{1,0:T(8,128)(2,1)} %get-tuple-element.4) | data formatting | bytes 983040
  57.3 0.0 copy-done
  57.3 0.6 %copy.10 = f32[10,192]{1,0:T(8,128)} copy(f32[10,192]{1,0:T(8,128)S(1)} %copy-done) | data formatting | bytes 15360
Async XLA Ops:
  55.4 1.9 %copy-start = (f32[10,192]{1,0:T(8,128)S(1)}, f32[10,192]{1,0:T(8,128)}, u32[]{:S(2)}) copy-start(f32[10,192]{1,0:T(8,128)} %get-tuple-element.5) | copy-start | bytes 23044

commit v2 on v1

--- a/solution.py
+++ b/solution.py
@@ -16,7 +16,7 @@
 BF16 = jnp.bfloat16
 SLOTS = {2: 3, 3: 2, 4: 1}
 PACK = {2: 144, 3: 80, 4: 48}
-BACK = {2: 64, 3: 48, 4: 32}
+BACK = {2: 64, 3: 32, 4: 16}
 OUT_ROWS = {2: 48, 3: 32, 4: 16}
 
 
@@ -67,10 +67,38 @@
     )
 
 
+def packed_lanes(level):
+    count = TOK // 2**level
+    lane = lax.broadcasted_iota(jnp.int32, (16, DH), 1).astype(F32)
+    return jnp.floor((lane + 0.5) * (1.0 / count))
+
+
+def pack_stats(lines, level, stride):
+    count = TOK // 2**level
+    wide = lines.shape[1]
+    lane = lax.broadcasted_iota(jnp.int32, (16, wide), 1).astype(F32)
+    row = lax.broadcasted_iota(jnp.int32, (16, wide), 0).astype(F32)
+    mine = jnp.floor((lane + 0.5) * (1.0 / stride)) == row
+    spread = jnp.concatenate([jnp.where(mine, lines[r : r + 1], 0.0) for r in range(9)], axis=0)
+    source = lax.broadcasted_iota(jnp.int32, (wide, DH), 0).astype(F32)
+    target = lax.broadcasted_iota(jnp.int32, (wide, DH), 1).astype(F32)
+    source = source - stride * jnp.floor((source + 0.5) * (1.0 / stride))
+    fold = jnp.where((source == target) & (target < count), 1.0, 0.0).astype(BF16)
+    moved = dot(spread.astype(BF16), fold, ((1,), (0,)))
+    room = DH // count
+    results = []
+    for first in range(0, 9, room):
+        total = moved[16 * first : 16 * first + 16]
+        for r in range(first + 1, min(first + room, 9)):
+            total = total + pltpu.roll(moved[16 * r : 16 * r + 16], count * (r - first), 1)
+        results.append(total)
+    return results
+
+
 def kernel(
-    offs, q_ref, k_ref, v_ref, gain_ref, out_ref, ent_ref,
+    offs, q_ref, k_ref, v_ref, plain, weight_ref, sway_ref, factor_ref,
     send1, send2, send3, send4, recv1, recv2, recv3, recv4, query1,
-    back2, back3, back4, ret2, ret3, ret4, stats, merged, plain, squares, others,
+    back2, back3, back4, ret2, ret3, ret4, stats, merged, squares, others,
     s1, s2, s3, s4, r1, r2, r3, r4, t2, t3, t4, u2, u3, u4, sq_sem,
 ):
     send, recv, back, ret = (
@@ -98,8 +126,7 @@
     def columns(h):
         return pl.ds(pl.multiple_of(h * DH, DH), DH)
 
-    @pl.loop(0, HEADS)
-    def _(h):
+    def pack(h):
         chosen = jnp.concatenate(
             [pick(1, offs[1, h], 96), pick(2, offs[2, h], 48), pick(3, offs[3, h], 24), pick(4, offs[4, h], 24)],
             axis=0,
@@ -116,8 +143,6 @@
         ).astype(BF16)
         send4[h] = jnp.concatenate([a[168:184] for a in (keys, vals, ques)], axis=0).astype(BF16)
 
-    pl.semaphore_wait(barrier, 16)
-
     def member(level):
         return lax.rem(seq, 2**level)
 
@@ -157,7 +182,13 @@
             device_id_type=MESH,
         )
 
-    for level in (2, 3, 4):
+    @pl.loop(0, HEADS, unroll=5)
+    def _(h):
+        pack(h)
+
+    pl.semaphore_wait(barrier, 16)
+
+    for level in (4, 3, 2):
 
         @pl.loop(0, HEADS)
         def _(h):
@@ -169,11 +200,7 @@
             def _():
                 recv[level][h // 2**level, member(level)] = send[level][h]
 
-    @pl.loop(0, HEADS)
-    def _(h):
-        near_copy(h).start()
-
-    @pl.loop(0, HEADS)
+    @pl.loop(0, HEADS, unroll=5)
     def _(h):
         peak, total, spread, weights = soft(k_ref[:, columns(h)], q_ref[:, columns(h)], 0)
         stats[h, 0:1] = peak
@@ -181,7 +208,7 @@
         stats[h, 2:3] = spread
         merged[h] = dot(v_ref[:, columns(h)], weights, ((0,), (0,)))
 
-    for level in (2, 3, 4):
+    for level in (4, 3, 2):
         group = 2**level
         rows = TOK // group
         for slot in range(SLOTS[level]):
@@ -228,15 +255,23 @@
                 peak, total, spread, weights = soft(keys, ques, level)
                 partial = dot(weights, vals, ((0,), (0,)))
                 lines = stat_rows((peak, total, spread))
-                if lines.shape[1] < 256:
-                    lines = jnp.concatenate([lines, jnp.zeros((16, 256 - lines.shape[1]), F32)], axis=1)
+                if level > 2:
+                    packed = pack_stats(lines, level, per)
+                else:
+                    lines = jnp.concatenate([lines, jnp.zeros((16, 256 - TOK), F32)], axis=1)
                 for m in range(group):
-                    turned = lines if m == 0 else pltpu.roll(lines, 256 - m * per, 1)
-                    pieces = [partial[m * per : m * per + per]]
+                    chunk = partial[m * per : m * per + per]
+                    if level == 2:
+                        turned = lines if m == 0 else pltpu.roll(lines, 256 - m * per, 1)
+                        chunk = jnp.concatenate([chunk, turned[:, 0:DH]], axis=0)
                     if level == 3:
-                        pieces.append(jnp.zeros((8, DH), F32))
-                    pieces.append(turned[:, 0:DH])
-                    back[level][slot, m] = jnp.concatenate(pieces, axis=0).astype(BF16)
+                        line = lax.broadcasted_iota(jnp.int32, (8, DH), 0)
+                        tail = jnp.where(line == 0, packed[0][m : m + 1], packed[1][m : m + 1])
+                        chunk = jnp.concatenate([chunk, tail], axis=0)
+                    if level == 4:
+                        line = lax.broadcasted_iota(jnp.int32, (16, DH), 0)
+                        chunk = jnp.where(line == rows, packed[0][m : m + 1], chunk)
+                    back[level][slot, m] = chunk.astype(BF16)
                 for m in range(group):
 
                     @pl.when(m != member(level))
@@ -247,6 +282,10 @@
                     def _():
                         ret[level][held] = back[level][slot, m]
 
+    @pl.loop(0, HEADS, unroll=5)
+    def _(h):
+        near_copy(h).start()
+
     def state(h):
         return stats[h, 0:1], stats[h, 1:2], stats[h, 2:3]
 
@@ -255,7 +294,63 @@
     def present(level, h):
         return (token & (2**level - 1)) == offs[level, h]
 
-    @pl.loop(0, HEADS)
+    stat_row = lax.broadcasted_iota(jnp.int32, (16, DH), 0).astype(F32)
+
+    def read_lines(level, h):
+        count = TOK // 2**level
+        spots = pick(level, offs[level, h], OUT_ROWS[level]).astype(BF16)
+        if level == 2:
+            every = pick(level, offs[level, h], DH).astype(BF16)
+            return dot(ret2[h, 48:64], every, ((1,), (0,))), spots
+        held = ret[level][h].astype(F32)
+        kind = packed_lanes(level)
+        room = DH // count
+        lines = jnp.where(kind == stat_row, held[count : count + 1], 0.0)
+        if room < 9:
+            lines = jnp.where((kind < room) & (stat_row < room), lines, 0.0)
+            lines = lines + jnp.where((kind < room) & (kind + room == stat_row), held[count + 1 : count + 2], 0.0)
+        lane = lax.broadcasted_iota(jnp.int32, (DH, TOK), 0).astype(F32)
+        token_of = lax.broadcasted_iota(jnp.int32, (DH, TOK), 1)
+        query = lane - count * jnp.floor((lane + 0.5) * (1.0 / count))
+        every = jnp.where(token_of == query.astype(jnp.int32) * 2**level + offs[level, h], 1.0, 0.0)
+        return dot(lines.astype(BF16), every.astype(BF16), ((1,), (0,))), spots
+
+    @pl.loop(0, HEADS, unroll=5)
+    def _(h):
+        for level in (2, 3, 4):
+
+            @pl.when(owner(level, h) != member(level))
+            def _():
+                pltpu.make_async_copy(back[level].at[0, 0], ret[level].at[h], ret_sem[level].at[h]).wait()
+
+        top, mass, moment = state(h)
+        new = top
+        found = []
+        for level in (2, 3, 4):
+            lines, spots = read_lines(level, h)
+            peak, total, spread = stat_values(lines)
+            there = present(level, h)
+            peak = jnp.where(there, peak, top)
+            new = jnp.maximum(new, peak)
+            part = dot(ret[level][h, 0 : OUT_ROWS[level]], spots, ((0,), (0,)))
+            found.append((there, peak, total, spread, part))
+        keep = jnp.exp(top - new)
+        weight = mass * keep
+        sway = keep * (moment + (top - new) * mass)
+        output = merged[h] * keep
+        for there, peak, total, spread, part in found:
+            fresh = jnp.where(there, jnp.exp(peak - new), 0.0)
+            weight = weight + total * fresh
+            sway = sway + fresh * (spread + (peak - new) * total)
+            output = output + part * fresh
+        stats[h, 0:1] = new
+        stats[h, 1:2] = weight
+        stats[h, 2:3] = sway
+        merged[h] = output
+
+    squares[...] = jnp.zeros_like(squares)
+
+    @pl.loop(0, HEADS, unroll=5)
     def _(h):
         near_copy(h).wait_recv()
         keys = jnp.concatenate([send1[h, 0:96], recv1[h, 0:96]], axis=0)
@@ -274,48 +369,11 @@
         new = jnp.maximum(top, peak)
         keep = jnp.exp(top - new)
         fresh = jnp.where(there, jnp.exp(peak - new), 0.0)
-        stats[h, 0:1] = new
-        stats[h, 1:2] = mass * keep + total * fresh
-        stats[h, 2:3] = keep * (moment + (top - new) * mass) + fresh * (spread + (peak - new) * total)
-        merged[h] = merged[h] * keep + (wide[0:DH] + wide[DH : 2 * DH]) * fresh
-
-    squares[...] = jnp.zeros_like(squares)
-
-    @pl.loop(0, HEADS)
-    def _(h):
-        for level in (2, 3, 4):
-
-            @pl.when(owner(level, h) != member(level))
-            def _():
-                pltpu.make_async_copy(back[level].at[0, 0], ret[level].at[h], ret_sem[level].at[h]).wait()
-
-        top, mass, moment = state(h)
-        new = top
-        found = []
-        for level in (2, 3, 4):
-            count = OUT_ROWS[level]
-            spots = pick(level, offs[level, h], DH).astype(BF16)
-            lines = dot(ret[level][h, count : count + 16], spots, ((1,), (0,)))
-            peak, total, spread = stat_values(lines)
-            there = present(level, h)
-            peak = jnp.where(there, peak, top)
-            new = jnp.maximum(new, peak)
-            part = dot(ret[level][h, 0:count], spots[0:count], ((0,), (0,)))
-            found.append((there, peak, total, spread, part))
-        keep = jnp.exp(top - new)
-        weight = mass * keep
-        sway = keep * (moment + (top - new) * mass)
-        factors = []
-        for there, peak, total, spread, part in found:
-            fresh = jnp.where(there, jnp.exp(peak - new), 0.0)
-            weight = weight + total * fresh
-            sway = sway + fresh * (spread + (peak - new) * total)
-            factors.append(fresh)
-        ent_ref[pl.ds(h, 1), :] = jnp.log(weight) - sway / weight
-        output = merged[h] * keep
-        for (there, peak, total, spread, part), fresh in zip(found, factors):
-            output = output + part * fresh
-        output = output * (1.0 / weight)
+        weight = mass * keep + total * fresh
+        weight_ref[pl.ds(h, 1), :] = weight
+        sway_ref[pl.ds(h, 1), :] = keep * (moment + (top - new) * mass) + fresh * (spread + (peak - new) * total)
+        scale = 1.0 / weight
+        output = merged[h] * (keep * scale) + (wide[0:DH] + wide[DH : 2 * DH]) * (fresh * scale)
         squares[0:1] += jnp.sum(output * output, axis=0, keepdims=True)
         plain[:, columns(h)] = jnp.transpose(output)
 
@@ -329,7 +387,7 @@
     )
     swap.start()
 
-    @pl.loop(0, HEADS)
+    @pl.loop(0, HEADS, unroll=5)
     def _(h):
         near_copy(h).wait_send()
         for level in (2, 3, 4):
@@ -352,11 +410,17 @@
     swap.wait()
     square = (squares[0:1] + others[0:1]) / (2 * HEADS * DH)
     factor = lax.rsqrt(square + 1e-06)
-    factor = jnp.transpose(jnp.broadcast_to(factor, (DH, TOK)))
-
-    @pl.loop(0, HEADS)
-    def _(h):
-        out_ref[:, columns(h)] = (plain[:, columns(h)] * factor * gain_ref[:, columns(h)]).astype(BF16)
+    factor_ref[...] = jnp.transpose(jnp.broadcast_to(factor, (DH, TOK)))
+
+
+def finish(plain_ref, factor_ref, gain_ref, weight_ref, sway_ref, out_ref, ent_ref):
+    factor = factor_ref[...]
+    for h in range(HEADS):
+        lanes = pl.ds(h * DH, DH)
+        gain = gain_ref[lanes].reshape(1, DH)
+        out_ref[:, lanes] = (plain_ref[:, lanes] * factor * gain).astype(BF16)
+    weight = weight_ref[...]
+    ent_ref[...] = jnp.log(weight) - sway_ref[...] / weight
 
 
 def shards(queries, keys, values, head_offsets, norm_gain):
@@ -377,7 +441,6 @@
     scratch += [
         pltpu.VMEM((HEADS, 8, TOK), F32),
         pltpu.VMEM((HEADS, DH, TOK), F32),
-        pltpu.VMEM((TOK, HEADS * DH), F32),
         pltpu.VMEM((8, TOK), F32),
         pltpu.VMEM((8, TOK), F32),
     ]
@@ -386,18 +449,30 @@
     scratch += [dma((SLOTS[k], 2**k)) for k in (2, 3, 4)]
     scratch += [dma((HEADS,)) for _ in range(3)]
     scratch += [dma((2,))]
+    plain, weight, sway, factor = pl.pallas_call(
+        kernel,
+        out_shape=(
+            jax.ShapeDtypeStruct((TOK, HEADS * DH), F32),
+            jax.ShapeDtypeStruct((HEADS, TOK), F32),
+            jax.ShapeDtypeStruct((HEADS, TOK), F32),
+            jax.ShapeDtypeStruct((TOK, DH), F32),
+        ),
+        in_specs=[smem, vmem, vmem, vmem],
+        out_specs=(vmem, vmem, vmem, vmem),
+        scratch_shapes=scratch,
+        compiler_params=pltpu.CompilerParams(collective_id=0, has_side_effects=True),
+        name="dilated",
+    )(head_offsets, queries, keys, values)
     return pl.pallas_call(
-        kernel,
+        finish,
         out_shape=(
             jax.ShapeDtypeStruct((TOK, HEADS * DH), BF16),
             jax.ShapeDtypeStruct((HEADS, TOK), F32),
         ),
-        in_specs=[smem, vmem, vmem, vmem, vmem],
+        in_specs=[vmem] * 5,
         out_specs=(vmem, vmem),
-        scratch_shapes=scratch,
-        compiler_params=pltpu.CompilerParams(collective_id=0, has_side_effects=True),
-        name="dilated",
-    )(head_offsets, queries, keys, values, norm_gain.reshape(1, HEADS * DH))
+        name="finish",
+    )(plain, factor, norm_gain, weight, sway)
 
 
 def solution(mesh):

time: 58.1 us -> 53.8 us (0.926)
  local copies, waits for them, and re-layouts: 3.75 us -> 0 us
  Pallas kernels: 53.5 us -> 52.6 us
    pallas_call x1, Pallas kernels: 53.5 us -> 50.4 us  [shards(): pl.pallas_call(kernel, out_shape=(jax.ShapeDtypeStruct((TOK, HEADS * DH),...]
    unnamed x4 -> x0, local copies, waits for them, and re-layouts: 2.45 us -> none
    pallas_call x0 -> x1, Pallas kernels: none -> 2.17 us  [shards(): pl.pallas_call(finish, out_shape=(jax.ShapeDtypeStruct((TOK, HEADS * DH),...]
    reshape x1 -> x0, local copies, waits for them, and re-layouts: 1.29 us -> none  [shards(): norm_gain.reshape(1, HEADS * DH)]
where the time goes in v2:
time: 53.8 us; the launch traced here: 53.2 us
  Pallas kernels  52.6 us (98%)
  between operations  0.64 us (1%)
    pallas_call x1, Pallas kernels, shards(): pl.pallas_call(kernel, out_shape=(jax.ShapeDtypeStruct((TOK, HEADS * DH),...  50.4 us
    pallas_call x1, Pallas kernels, shards(): pl.pallas_call(finish, out_shape=(jax.ShapeDtypeStruct((TOK, HEADS * DH),...  2.17 us

profile of v2, /device:TPU:1, one launch (start us, length us, event | category | flops | bytes accessed | tf_op | source)
XLA Modules:
  0.0 53.2 jit_solution(6233463547475565088)
XLA Ops:
  0.6 50.4 %dilated.1 = (f32[192,1280]{1,0:T(8,128)}, f32[10,192]{1,0:T(8,128)}, f32[10,192]{1,0:T(8,128)}, f32[192,128]{1,0:T(8,128)}) custom-call(s32[5,10]{1,0:T(8,128)} %offs.1, bf16[192,1280]{1,0:T(8,128)(2,1)} %q_ref.1, bf16[192,1280]{1,0:T(8,128)(2,1)} %k_ref.1, bf16[192,1280]{1,0:T(8,128)(2,1)} %v_ref.1), custom_call_target="tpu_custom_call" | custom-call | tf_op jit(solution)/shard_map/dilated/pallas_call | solution.py:452
  51.0 2.2 %finish.1 = (bf16[192,1280]{1,0:T(8,128)(2,1)}, f32[10,192]{1,0:T(8,128)}) custom-call(f32[192,1280]{1,0:T(8,128)} %get-tuple-element.6.plain_ref, f32[192,128]{1,0:T(8,128)} %get-tuple-element.7.factor_ref, f32[1280]{0:T(1024)} %gain_ref.1, f32[10,192]{1,0:T(8,128)} %get-tuple-element.8.weight_ref, f32[10,192]{1,0:T(8,128)} %get-tuple-element.9.sway_ref), custom_call_target="tpu_custom_call" | custom-call | tf_op jit(solution)/shard_map/finish/pallas_call | solution.py:466

commit v3 on v2

--- a/solution.py
+++ b/solution.py
@@ -11,11 +11,13 @@
 TOK = 192
 HEADS = 10
 LEVELS = 5
+FINISH = 640
 MESH = pl.DeviceIdType.MESH
 F32 = jnp.float32
 BF16 = jnp.bfloat16
 SLOTS = {2: 3, 3: 2, 4: 1}
 PACK = {2: 144, 3: 80, 4: 48}
+SENT = {2: 144, 3: 72, 4: 48}
 BACK = {2: 64, 3: 32, 4: 16}
 OUT_ROWS = {2: 48, 3: 32, 4: 16}
 
@@ -154,8 +156,8 @@
 
     def pack_copy(level, h):
         return pltpu.make_async_remote_copy(
-            src_ref=send[level].at[h],
-            dst_ref=recv[level].at[h // 2**level, member(level)],
+            src_ref=send[level].at[h, pl.ds(0, SENT[level])],
+            dst_ref=recv[level].at[h // 2**level, member(level), pl.ds(0, SENT[level])],
             send_sem=send_sem[level].at[h],
             recv_sem=recv_sem[level].at[h // 2**level, member(level)],
             device_id={"seq": seq - member(level) + owner(level, h), "head": core},
@@ -182,15 +184,8 @@
             device_id_type=MESH,
         )
 
-    @pl.loop(0, HEADS, unroll=5)
-    def _(h):
-        pack(h)
-
-    pl.semaphore_wait(barrier, 16)
-
-    for level in (4, 3, 2):
-
-        @pl.loop(0, HEADS)
+    def send_packs(level, first, last):
+        @pl.loop(first, last)
         def _(h):
             @pl.when(owner(level, h) != member(level))
             def _():
@@ -199,6 +194,24 @@
             @pl.when(owner(level, h) == member(level))
             def _():
                 recv[level][h // 2**level, member(level)] = send[level][h]
+
+    half = HEADS // 2
+
+    @pl.loop(0, half, unroll=5)
+    def _(h):
+        pack(h)
+
+    pl.semaphore_wait(barrier, 16)
+    send_packs(4, 0, half)
+    send_packs(3, 0, half)
+
+    @pl.loop(half, HEADS, unroll=5)
+    def _(h):
+        pack(h)
+
+    send_packs(4, half, HEADS)
+    send_packs(3, half, HEADS)
+    send_packs(2, 0, HEADS)
 
     @pl.loop(0, HEADS, unroll=5)
     def _(h):
@@ -221,7 +234,7 @@
                     @pl.when(m != member(level))
                     def _():
                         pltpu.make_async_copy(
-                            send[level].at[0], recv[level].at[slot, m], recv_sem[level].at[slot, m]
+                            send[level].at[0, pl.ds(0, SENT[level])], recv[level].at[slot, m, pl.ds(0, SENT[level])], recv_sem[level].at[slot, m]
                         ).wait()
 
                 if level == 4:
@@ -415,12 +428,15 @@
 
 def finish(plain_ref, factor_ref, gain_ref, weight_ref, sway_ref, out_ref, ent_ref):
     factor = factor_ref[...]
-    for h in range(HEADS):
+    for h in range(FINISH // DH):
         lanes = pl.ds(h * DH, DH)
-        gain = gain_ref[lanes].reshape(1, DH)
+        gain = gain_ref[pl.ds(pl.multiple_of(pl.program_id(0) * FINISH + h * DH, DH), DH)].reshape(1, DH)
         out_ref[:, lanes] = (plain_ref[:, lanes] * factor * gain).astype(BF16)
-    weight = weight_ref[...]
-    ent_ref[...] = jnp.log(weight) - sway_ref[...] / weight
+
+    @pl.when(pl.program_id(0) == 0)
+    def _():
+        weight = weight_ref[...]
+        ent_ref[...] = jnp.log(weight) - sway_ref[...] / weight
 
 
 def shards(queries, keys, values, head_offsets, norm_gain):
@@ -469,8 +485,18 @@
             jax.ShapeDtypeStruct((TOK, HEADS * DH), BF16),
             jax.ShapeDtypeStruct((HEADS, TOK), F32),
         ),
-        in_specs=[vmem] * 5,
-        out_specs=(vmem, vmem),
+        grid=(HEADS * DH // FINISH,),
+        in_specs=[
+            pl.BlockSpec((TOK, FINISH), lambda i: (0, i)),
+            pl.BlockSpec((TOK, DH), lambda i: (0, 0)),
+            vmem,
+            pl.BlockSpec((HEADS, TOK), lambda i: (0, 0)),
+            pl.BlockSpec((HEADS, TOK), lambda i: (0, 0)),
+        ],
+        out_specs=(
+            pl.BlockSpec((TOK, FINISH), lambda i: (0, i)),
+            pl.BlockSpec((HEADS, TOK), lambda i: (0, 0)),
+        ),
         name="finish",
     )(plain, factor, norm_gain, weight, sway)
 

time: 53.8 us -> 53.4 us (level)
  no operation moved by 1% of the time
where the time goes in v3:
time: 53.4 us; the launch traced here: 53.2 us
  Pallas kernels  52.6 us (99%)
  between operations  0.64 us (1%)
    pallas_call x1, Pallas kernels, shards(): pl.pallas_call(kernel, out_shape=(jax.ShapeDtypeStruct((TOK, HEADS * DH),...  50.5 us
    pallas_call x1, Pallas kernels, shards(): pl.pallas_call(finish, out_shape=(jax.ShapeDtypeStruct((TOK, HEADS * DH),...  2.06 us

profile of v3, /device:TPU:1, one launch (start us, length us, event | category | flops | bytes accessed | tf_op | source)
XLA Modules:
  0.0 53.2 jit_solution(8234431514920799953)
XLA Ops:
  0.6 50.5 %dilated.1 = (f32[192,1280]{1,0:T(8,128)}, f32[10,192]{1,0:T(8,128)}, f32[10,192]{1,0:T(8,128)}, f32[192,128]{1,0:T(8,128)}) custom-call(s32[5,10]{1,0:T(8,128)} %offs.1, bf16[192,1280]{1,0:T(8,128)(2,1)} %q_ref.1, bf16[192,1280]{1,0:T(8,128)(2,1)} %k_ref.1, bf16[192,1280]{1,0:T(8,128)(2,1)} %v_ref.1), custom_call_target="tpu_custom_call" | custom-call | tf_op jit(solution)/shard_map/dilated/pallas_call | solution.py:468
  51.1 2.1 %finish.1 = (bf16[192,1280]{1,0:T(8,128)(2,1)}, f32[10,192]{1,0:T(8,128)}) custom-call(f32[192,1280]{1,0:T(8,128)} %get-tuple-element.6.plain_ref, f32[192,128]{1,0:T(8,128)} %get-tuple-element.7.factor_ref, f32[1280]{0:T(1024)} %gain_ref.1, f32[10,192]{1,0:T(8,128)} %get-tuple-element.8.weight_ref, f32[10,192]{1,0:T(8,128)} %get-tuple-element.9.sway_ref), custom_call_target="tpu_custom_call" | custom-call | tf_op jit(solution)/shard_map/finish/pallas_call | solution.py:482
